TPU v7x, 256 devices: a whole 4x4x8 slice. The times are simulated.
256 devices in a mesh: ctx: 32 (over z_lo, x, core), wt: 8 (over y, z_hi).
Axes of the slice: x: 4, y: 4, z: 8 (z_hi: 2, z_lo: 4; z = z_hi * 4 + z_lo), core: 2. Of those that a mesh axis runs over, the one named last changes fastest.
Arguments:
- patches: bfloat16 [16384, 1280], P('ctx'), may hold values from -6 to 6
- vit_gain: float32 [1280], replicated, may hold values from 0.5 to 1.5
- vit_codes: bfloat16 [1280, 3, 1280], P(None, None, 'wt'), may hold values from -1 to 1
- vit_scales: bfloat16 [8], P('wt'), may hold values from 0.5 to 2
- vit_bias: float32 [3, 1280], P(None, 'wt'), may hold values from -3 to 3
- window_ids: int32 [16384], P('ctx'), may hold values from 63 to 16383, as said below
- merger_codes: bfloat16 [4, 1280, 8192], P(None, 'wt', 'ctx'), may hold values from -0.078125 to 0.078125
- merger_scales: bfloat16 [1, 8, 8192], P(None, 'wt', 'ctx'), may hold values from 0.5 to 2
- merger_bias: float32 [8192], P('wt'), may hold values from -3 to 3
- positions: int32 [4096], P('ctx'), may hold values from 0 to 16383, as said below
- text_embed: bfloat16 [16384, 8192], P('ctx', 'wt'), may hold values from -6 to 6
- norm_gain: float32 [8192], P('wt'), may hold values from 0.5 to 1.5
- llm_codes: bfloat16 [8192, 8, 768], P('wt', None, 'ctx'), may hold values from -1 to 1
- llm_scales: bfloat16 [8, 8, 768], P('wt', None, 'ctx'), may hold values from 0.5 to 2
- llm_bias: float32 [8, 768], P('wt'), may hold values from -3 to 3
- segments: int32 [16384], P('ctx'), may hold values from 0 to 15, never falling along the last dimension, each value on 1 to 2048 neighbouring positions
Outputs:
- attention_out: bfloat16 [16384, 4096], P('ctx', 'wt')
Inputs may be any that keep to these rules, and one draw needn't show every extreme that they name: `window_ids`: windows are runs of consecutive patches of at most 64, never crossing a block of 512 patches; patches of one window share the id, different windows have different ids. `positions`: distinct. The 128 entries of one aligned block (one device's merged tokens) put at most 8 into any one block of 512 positions, and exactly 8 into some block. `segments`: never falling; each run of equal ids is at most 2048 positions long.
All inputs are finite; a program needn't handle non-finite values.
Results may differ from a plain program's by a relative error of at most 0.025.
Values may be sent and summed in bfloat16 or wider, within the bound.
A program may use at most 128 MiB of HBM per device.

v0:
```python
import jax
import jax.numpy as jnp
from jax import lax
from jax.sharding import PartitionSpec as P

VHD = 80
D = 8192
KVH = 8
HD = 128
GROUP = 4
MERGE = 4
REACH = 4
VIT_EPS = 1e-06
RMS_EPS = 1e-06
ROPE_BASE = 1000000.0
FILL_LOW = -1e30


def in_blocks(x, dim, peers):
    before, after = (x.shape[:dim], x.shape[dim + 1 :])
    return jnp.moveaxis(x.reshape(*before, peers, -1, *after), dim, 0)


def summed_on_arrival(x, axis, dim):
    parts = in_blocks(x, dim, lax.axis_size(axis))
    arrived = lax.all_to_all(parts, axis, split_axis=0, concat_axis=0, tiled=True)
    return arrived.astype(jnp.float32).sum(axis=0)


def passed_along(value, axis, steps):
    count = lax.axis_size(axis)
    leading, last = (max(0, -steps), min(count, count - steps))
    return lax.ppermute(value, axis, [(source, source + steps) for source in range(leading, last)])


def softmax_rows(scores, allowed):
    masked = jnp.where(allowed, scores, FILL_LOW)
    highest = jnp.max(masked, axis=-1, keepdims=True)
    raised = jnp.exp(masked - highest)
    return raised / jnp.sum(raised, axis=-1, keepdims=True)


def vision_norm_rows(patches, vit_gain):
    values = patches.astype(jnp.float32)
    mean_square = jnp.mean(values * values, axis=1, keepdims=True)
    return (values * lax.rsqrt(mean_square + VIT_EPS) * vit_gain).astype(jnp.bfloat16)


def window_attention(normed, weight_block, bias_block, window_ids):
    row_count = normed.shape[0]
    packed = jnp.dot(
        normed, weight_block.reshape(normed.shape[1], -1), preferred_element_type=jnp.float32
    )
    triple = (packed.reshape(row_count, 3, -1) + bias_block).astype(jnp.bfloat16)
    heads_here = triple.shape[2] // VHD
    queries = triple[:, 0].reshape(row_count, heads_here, VHD)
    keys_here = triple[:, 1].reshape(row_count, heads_here, VHD)
    values_here = triple[:, 2].reshape(row_count, heads_here, VHD)
    scores = jnp.einsum(
        "qhd,khd->hqk", queries, keys_here, preferred_element_type=jnp.float32
    ) * VHD ** (-0.5)
    allowed = window_ids[:, None] == window_ids[None, :]
    softmaxed = softmax_rows(scores, allowed[None]).astype(jnp.bfloat16)
    blended = jnp.einsum("hqk,khd->qhd", softmaxed, values_here, preferred_element_type=jnp.float32)
    return blended.astype(jnp.bfloat16).reshape(row_count, -1)


def rope_tables(first, length):
    places = (first + jnp.arange(length, dtype=jnp.int32)).astype(jnp.float32)
    frequency = ROPE_BASE ** (-jnp.arange(0, HD, 2).astype(jnp.float32) / HD)
    angles = places[:, None] * frequency[None, :]
    angles = jnp.concatenate([angles, angles], axis=1)
    return (jnp.cos(angles), jnp.sin(angles))


def rotary(inputs, cosine, sine):
    halfway = inputs.shape[-1] // 2
    turned = jnp.concatenate([-inputs[..., halfway:], inputs[..., :halfway]], axis=-1)
    return inputs * cosine + turned * sine


def split_heads(triple, cosine, sine):
    row_count, group_count = (triple.shape[0], triple.shape[1])
    queries = triple[:, :, : GROUP * HD].reshape(row_count, group_count, GROUP, HD)
    queries = rotary(queries, cosine[:, None, None, :], sine[:, None, None, :]).astype(jnp.bfloat16)
    keys_rot = rotary(
        triple[:, :, GROUP * HD : (GROUP + 1) * HD], cosine[:, None, :], sine[:, None, :]
    ).astype(jnp.bfloat16)
    values_cut = triple[:, :, (GROUP + 1) * HD :].astype(jnp.bfloat16)
    return (queries, keys_rot, values_cut)


def merge_project(features, merger_codes, merger_scales, merger_bias):
    row_count = features.shape[0]
    flat = features.reshape(row_count, -1)
    codes_piece = lax.all_gather(merger_codes, "ctx", axis=2, tiled=True)
    scale_piece = lax.all_gather(merger_scales, "ctx", axis=2, tiled=True)
    width = codes_piece.shape[2]
    dequant = (codes_piece.astype(jnp.float32) * scale_piece.astype(jnp.float32)).astype(
        jnp.bfloat16
    )
    product = jnp.dot(flat, dequant.reshape(-1, width), preferred_element_type=jnp.float32)
    mine = summed_on_arrival(product.astype(jnp.bfloat16), "wt", 1)
    return (mine + merger_bias).astype(jnp.bfloat16)


def route_tokens(values, positions, span):
    owners = lax.axis_size("ctx")
    items = values.shape[0]
    capacity = 2 * positions.shape[0] // owners
    target = positions // span
    item_order = jnp.arange(items, dtype=jnp.int32)
    before = (target[None, :] == target[:, None]) & (item_order[None, :] < item_order[:, None])
    ranks = jnp.sum(before.astype(jnp.int32), axis=1)
    slots = target * capacity + ranks
    table = slots[None, :] == jnp.arange(owners * capacity, dtype=jnp.int32)[:, None]
    packed = jnp.dot(table.astype(jnp.bfloat16), values, preferred_element_type=jnp.float32).astype(
        jnp.bfloat16
    )
    labels = jnp.sum(jnp.where(table, positions[None, :] + 1, 0), axis=1) - 1
    return (
        lax.all_to_all(packed, "ctx", split_axis=0, concat_axis=0, tiled=True),
        lax.all_to_all(labels, "ctx", split_axis=0, concat_axis=0, tiled=True),
    )


def place_tokens(text_embed, arrived, labels, first):
    local = labels - first
    table = local[None, :] == jnp.arange(text_embed.shape[0], dtype=jnp.int32)[:, None]
    filled = jnp.dot(
        table.astype(jnp.bfloat16), arrived, preferred_element_type=jnp.float32
    ).astype(jnp.bfloat16)
    covered = jnp.any(table, axis=1)
    return jnp.where(covered[:, None], filled, text_embed)


def on_device(
    patches,
    vit_gain,
    vit_codes,
    vit_scales,
    vit_bias,
    window_ids,
    merger_codes,
    merger_scales,
    merger_bias,
    positions,
    text_embed,
    norm_gain,
    llm_codes,
    llm_scales,
    llm_bias,
    segments,
):
    early_codes, early_scales = (
        lax.all_gather(llm_codes, "ctx", axis=2, tiled=True),
        lax.all_gather(llm_scales, "ctx", axis=2, tiled=True),
    )
    row_count = text_embed.shape[0]
    first = lax.axis_index("ctx") * row_count
    normed_patches = vision_norm_rows(patches, vit_gain)
    vit_weight = (vit_codes.astype(jnp.float32) * vit_scales.astype(jnp.float32)[0]).astype(
        jnp.bfloat16
    )
    attended = window_attention(normed_patches, vit_weight, vit_bias, window_ids)
    token_count = positions.shape[0]
    features = attended.reshape(token_count, MERGE, -1)
    projected = merge_project(features, merger_codes, merger_scales, merger_bias)
    embedded, labels = route_tokens(projected, positions, row_count)
    hidden = place_tokens(text_embed, embedded, labels, first)
    values = hidden.astype(jnp.float32)
    squares = lax.psum(jnp.sum(values * values, axis=1), "wt")
    normed = (values * lax.rsqrt(squares[:, None] / D + RMS_EPS) * norm_gain).astype(jnp.bfloat16)
    local_rows = normed.shape[1]
    dequant = (early_codes.astype(jnp.float32) * early_scales.astype(jnp.float32)).astype(
        jnp.bfloat16
    )
    partial_value = jnp.dot(
        normed, dequant.reshape(local_rows, -1), preferred_element_type=jnp.float32
    ).reshape(row_count, KVH, -1)
    triple = (
        lax.psum_scatter(
            partial_value.astype(jnp.bfloat16), "wt", scatter_dimension=1, tiled=True
        ).astype(jnp.float32)
        + llm_bias
    )
    cosine, sine = rope_tables(first, row_count)
    queries, keys_rot, values_cut = split_heads(triple, cosine, sine)
    own = (keys_rot, values_cut, segments)
    arrivals = [own]
    for distance in range(1, REACH + 1):
        arrivals.append(passed_along((own[0], own[1], own[2]), "ctx", distance))
    keys_all = jnp.concatenate([arrival[0] for arrival in arrivals], axis=0)
    values_all = jnp.concatenate([arrival[1] for arrival in arrivals], axis=0)
    key_segments = jnp.concatenate([arrival[2] for arrival in arrivals], axis=0)
    key_places = jnp.concatenate(
        [
            first - distance * row_count + jnp.arange(row_count, dtype=jnp.int32)
            for distance in range(REACH + 1)
        ],
        axis=0,
    )
    query_places = first + jnp.arange(row_count, dtype=jnp.int32)
    allowed = (
        (segments[:, None] == key_segments[None, :])
        & (key_places[None, :] <= query_places[:, None])
        & (key_places[None, :] >= 0)
    )
    scores = jnp.einsum(
        "qjd,kd->jqk", queries[:, 0], keys_all[:, 0], preferred_element_type=jnp.float32
    ) * HD ** (-0.5)
    softmaxed = softmax_rows(scores, allowed[None]).astype(jnp.bfloat16)
    blended = jnp.einsum(
        "jqk,kd->qjd", softmaxed, values_all[:, 0], preferred_element_type=jnp.float32
    )
    outputs = blended.astype(jnp.bfloat16).reshape(row_count, -1)
    return outputs


def solution(mesh):
    in_specs = (
        P("ctx", None),
        P(),
        P(None, None, "wt"),
        P("wt"),
        P(None, "wt"),
        P("ctx"),
        P(None, "wt", "ctx"),
        P(None, "wt", "ctx"),
        P("wt"),
        P("ctx"),
        P("ctx", "wt"),
        P("wt"),
        P("wt", None, "ctx"),
        P("wt", None, "ctx"),
        P("wt", None),
        P("ctx"),
    )
    out_specs = P("ctx", "wt")
    return jax.shard_map(
        on_device, mesh=mesh, in_specs=in_specs, out_specs=out_specs, check_vma=False
    )
```

profile of v0, /device:TPU:1, one launch (start us, length us, event | category | flops | bytes accessed | tf_op | source)
XLA Modules:
  0.0 532.9 jit_solution(2838187777075380373)
XLA Ops:
  8.7 1.6 fusion.14
  11.3 2.2 fusion.29
  16.2 45.9 %all_gather.13 = bf16[1,1,8192]{2,1,0:T(2,128)(2,1)S(1)} all-gather(bf16[1,1,256]{2,1,0:T(2,128)(2,1)S(1)} %copy-done.8), channel_id=1, replica_groups=mesh['ctx'=32,'wt'=8] {'ctx'}, dimensions={2}, use_global_device_ids=true | all-gather | bytes 16896 | tf_op jit(solution)/shard_map/all_gather | solution.py:97
  62.2 47.2 %all-gather.3.cloned.1.call-done = bf16[4,160,8192]{2,1,0:T(8,128)(2,1)} async-done(((bf16[4,160,256]{2,1,0:T(8,128)(2,1)}), bf16[4,160,8192]{2,1,0:T(8,128)(2,1)}) %all-gather.3.cloned.1.call-update) | async-done | bytes 10485776 | tf_op jit(solution)/shard_map/all_gather | solution.py:96
  109.4 6.2 %multiply_convert_fusion.1 = bf16[4,160,8192]{2,1,0:T(8,128)(2,1)S(1)} fusion(bf16[4,160,8192]{2,1,0:T(8,128)(2,1)} %all-gather.3.cloned.1.call-done, f32[8192]{0:T(1024)S(1)} %bitcast.110), kind=kLoop, calls=%fused_computation.6 | loop fusion | flops 15728640 | bytes 21004288 | tf_op jit(solution)/shard_map/convert_element_type | solution.py:99
  115.6 2.0 convolution_convert_fusion
  119.1 7.4 %all-to-all-start.1 = ((bf16[8,128,1024]{2,1,0:T(8,128)(2,1)}), bf16[8,128,1024]{2,1,0:T(8,128)(2,1)S(1)}, u32[]{:S(2)}, u32[]{:S(2)}) async-start(bf16[8,128,1024]{2,1,0:T(8,128)(2,1)} %bitcast.102), calls=%async_computation.1 | async-start | bytes 4194304 | tf_op jit(solution)/shard_map/all_to_all | solution.py:26
  127.6 74.6 %all-to-all-done.1 = bf16[8,128,1024]{2,1,0:T(8,128)(2,1)S(1)} async-done(((bf16[8,128,1024]{2,1,0:T(8,128)(2,1)}), bf16[8,128,1024]{2,1,0:T(8,128)(2,1)S(1)}, u32[]{:S(2)}, u32[]{:S(2)}) %all-to-all-start.1) | async-done | bytes 2097184 | tf_op jit(solution)/shard_map/all_to_all | solution.py:26
  202.2 4.9 all-to-all-start
  208.6 6.0 %all-to-all-done = s32[32,8,1]{1,2,0:T(1,128)S(1)} async-done(((s32[32,8,1]{1,2,0:T(1,128)}), s32[32,8,1]{1,2,0:T(1,128)S(1)}, u32[]{:S(2)}, u32[]{:S(2)}) %all-to-all-start) | async-done | bytes 1056 | tf_op jit(solution)/shard_map/all_to_all | solution.py:123
  214.6 4.1 all-to-all-start.2
  218.9 54.9 %all_gather.15 = bf16[1,8,768]{1,0,2:T(2,128)(2,1)S(1)} all-gather(bf16[1,8,24]{1,0,2:T(2,128)(2,1)S(1)} %copy.42), channel_id=1, replica_groups=mesh['ctx'=32,'wt'=8] {'ctx'}, dimensions={2}, use_global_device_ids=true | all-gather | bytes 12672 | tf_op jit(solution)/shard_map/all_gather | solution.py:157
  275.3 22.5 %psum.7 = f32[512]{0:T(512)S(1)} all-reduce(f32[512]{0:T(512)S(1)} %get-tuple-element.24), channel_id=1, replica_groups=mesh['ctx'=32,'wt'=8] {'wt'}, use_global_device_ids=true, to_apply=%region_8.9 | all-reduce | flops 512 | bytes 4096 | tf_op jit(solution)/shard_map/psum | solution.py:172
  297.8 11.6 %fusion.11 = bf16[512,8,768]{2,0,1:T(8,128)(2,1)} fusion(bf16[1024,8,768]{0,2,1:T(8,128)(2,1)} %all-gather.5.cloned.1.call-done, f32[8,768]{1,0:T(8,128)S(1)} %copy.43, bf16[512,1024]{1,0:T(8,128)(2,1)S(1)} %get-tuple-element.25, f32[1024]{0:T(1024)S(1)} %copy-done.12, f32[512]{0:T(512)S(1)} %add_rsqrt_fusion), kind=kOutput, calls=%fused_computation.18 | convolution fusion | flops 6466568192 | bytes 19953664 | tf_op jit(solution)/shard_map/dot_general | solution.py:178
  310.1 4.9 collective-permute-start.4
  317.6 1.6 collective-permute-start.7
  322.3 3.5 and_and_fusion
  325.8 132.5 %reduce-scatter.2.cloned.1.call-done = bf16[512,1,768]{2,0,1:T(8,128)(2,1)} async-done(((bf16[512,8,768]{2,0,1:T(8,128)(2,1)}), bf16[512,1,768]{2,0,1:T(8,128)(2,1)}) %reduce-scatter.2.cloned.1.call-update) | async-done | bytes 786448 | tf_op jit(solution)/shard_map/reduce_scatter | solution.py:182
  459.6 1.9 constant_dynamic-update-slice_fusion.4
  461.6 5.8 %collective-permute-start = (bf16[512,1,128]{2,0,1:T(8,128)(2,1)}, bf16[512,1,128]{2,0,1:T(8,128)(2,1)S(1)}, u32[]{:S(2)}, u32[]{:S(2)}) collective-permute-start(bf16[512,1,128]{2,0,1:T(8,128)(2,1)} %get-tuple-element.6), channel_id=1, source_target_pairs={{0,8},{8,16},{16,24},{24,32},{32,40},{40,48},{48,56},{56,64},{64,7... | collective-permute-start | bytes 393224 | tf_op jit(solution)/shard_map/ppermute | solution.py:33
  467.3 3.1 collective-permute-start.1
  470.4 3.4 collective-permute-start.2
  475.0 2.5 collective-permute-start.8
  477.5 3.8 collective-permute-start.9
  483.5 1.6 maximum_multiply_fusion
  485.2 2.6 mul.223
  489.4 3.3 collective-permute-start.10
  494.3 2.4 collective-permute-start.11
  496.7 1.6 constant_dynamic-update-slice_fusion.9
  498.2 4.5 collective-permute-start.3
  504.1 12.6 %fusion.83 = (f32[4,512]{1,0:T(4,128)S(1)}, f32[4,512,2560]{1,2,0:T(8,128)}) fusion(pred[512,2560]{0,1:T(8,128)(4,1)S(1)} %copy-done.2, bf16[2560,1,128]{2,0,1:T(8,128)(2,1)} %constant_dynamic-update-slice_fusion.7, bf16[512,4,128]{2,1,0:T(4,128)(2,1)S(1)} %convert_element_type.133), kind=kOutput, calls=%fused_computation.137 | convolution fusion | flops 1363151360 | bytes 23470080 | tf_op jit(solution)/shard_map/sub | solution.py:39
  516.9 8.5 %fusion.28 = bf16[128,4,512]{2,0,1:T(8,128)(2,1)S(1)} fusion(f32[4,512,2560]{1,2,0:T(8,128)} %get-tuple-element.27, f32[4,512]{1,0:T(4,128)S(1)} %get-tuple-element.26, bf16[2560,1,128]{2,0,1:T(8,128)(2,1)S(1)} %constant_dynamic-update-slice_fusion), kind=kOutput, calls=%fused_computation.44 | convolution fusion | flops 1352925184 | bytes 22159360 | tf_op jit(solution)/shard_map/jqk,kd->qjd/dot_general | solution.py:213
  (110 shorter events, 27.2 us)
Async XLA Ops:
  6.5 4.8 copy-start.1
  6.5 4.8 copy-start.10
  6.5 4.8 copy-start.11
  6.5 102.9 %all-gather.3.cloned.1.call-start = ((), (), s32[]{:S(2)}) async-start(), calls=%async_computation.4 | async-start | bytes 10813440 | tf_op jit(solution)/shard_map/all_gather | solution.py:96
  7.3 290.5 %all-gather.5.cloned.1.call-start = ((), (), s32[]{:S(2)}) async-start(), calls=%async_computation.5 | async-start | bytes 12976128 | tf_op jit(solution)/shard_map/all_gather | solution.py:156
  14.6 1.6 copy-start.8
  119.1 7.4 %copy-start.13 = (s32[128]{0:T(128)S(1)}, s32[128]{0:T(128)}, u32[]{:S(2)}) copy-start(s32[128]{0:T(128)} %param.25) | copy-start | bytes 1540
  119.1 83.1 %all-to-all-start.1 = ((bf16[8,128,1024]{2,1,0:T(8,128)(2,1)}), bf16[8,128,1024]{2,1,0:T(8,128)(2,1)S(1)}, u32[]{:S(2)}, u32[]{:S(2)}) async-start(bf16[8,128,1024]{2,1,0:T(8,128)(2,1)} %bitcast.102), calls=%async_computation.1 | async-start | bytes 4194304 | tf_op jit(solution)/shard_map/all_to_all | solution.py:26
  126.5 81.0 %copy-start.5 = (f32[1024]{0:T(1024)S(1)}, f32[1024]{0:T(1024)}, u32[]{:S(2)}) copy-start(f32[1024]{0:T(1024)} %param.24) | copy-start | bytes 12292
  202.2 12.4 %all-to-all-start = ((s32[32,8,1]{1,2,0:T(1,128)}), s32[32,8,1]{1,2,0:T(1,128)S(1)}, u32[]{:S(2)}, u32[]{:S(2)}) async-start(s32[32,8,1]{1,2,0:T(1,128)} %bitcast), calls=%async_computation | async-start | bytes 32768 | tf_op jit(solution)/shard_map/all_to_all | solution.py:123
  207.1 11.6 %copy-start.7 = (bf16[1,8,24]{2,1,0:T(8,128)(2,1)S(1)}, bf16[1,8,24]{2,1,0:T(8,128)(2,1)}, u32[]{:S(2)}) copy-start(bf16[1,8,24]{2,1,0:T(8,128)(2,1)} %param.29) | copy-start | bytes 1156
  207.5 67.2 %copy-start.9 = (bf16[512,1024]{1,0:T(8,128)(2,1)S(1)}, bf16[512,1024]{1,0:T(8,128)(2,1)}, u32[]{:S(2)}) copy-start(bf16[512,1024]{1,0:T(8,128)(2,1)} %param.26) | copy-start | bytes 3145732
  214.6 60.0 %all-to-all-start.2 = ((bf16[32,8,1024]{2,1,0:T(8,128)(2,1)}), bf16[32,8,1024]{2,1,0:T(8,128)(2,1)S(1)}, u32[]{:S(2)}, u32[]{:S(2)}) async-start(bf16[32,8,1024]{2,1,0:T(8,128)(2,1)} %fusion.32), calls=%async_computation.2 | async-start | bytes 1048576 | tf_op jit(solution)/shard_map/all_to_all | solution.py:122
  218.7 239.6 %reduce-scatter.2.cloned.1.call-start = ((), (), s32[]{:S(2)}) async-start(), calls=%async_computation.6 | async-start | bytes 7077888 | tf_op jit(solution)/shard_map/reduce_scatter | solution.py:182
  274.2 23.6 %copy-start.12 = (f32[1024]{0:T(1024)S(1)}, f32[1024]{0:T(1024)}, u32[]{:S(2)}) copy-start(f32[1024]{0:T(1024)} %param.27) | copy-start | bytes 12292
  309.4 0.7 copy-start.4
  310.1 12.1 %collective-permute-start.4 = (s32[512]{0:T(512)S(1)}, s32[512]{0:T(512)S(1)}, u32[]{:S(2)}, u32[]{:S(2)}) collective-permute-start(s32[512]{0:T(512)S(1)} %copy-done.4), channel_id=1, source_target_pairs={{0,8},{8,16},{16,24},{24,32},{32,40},{40,48},{48,56},{56,64},{64,7... | collective-permute-start | bytes 6152 | tf_op jit(solution)/shard_map/ppermute | solution.py:33
  315.0 7.3 %collective-permute-start.5 = (s32[512]{0:T(512)S(1)}, s32[512]{0:T(512)S(1)}, u32[]{:S(2)}, u32[]{:S(2)}) collective-permute-start(s32[512]{0:T(512)S(1)} %copy-done.4), channel_id=1, source_target_pairs={{0,16},{8,24},{16,32},{24,40},{32,48},{40,56},{48,64},{56,72},{64,... | collective-permute-start | bytes 6152 | tf_op jit(solution)/shard_map/ppermute | solution.py:33
  316.3 6.0 %collective-permute-start.6 = (s32[512]{0:T(512)S(1)}, s32[512]{0:T(512)S(1)}, u32[]{:S(2)}, u32[]{:S(2)}) collective-permute-start(s32[512]{0:T(512)S(1)} %copy-done.4), channel_id=1, source_target_pairs={{0,24},{8,32},{16,40},{24,48},{32,56},{40,64},{48,72},{56,80},{64,... | collective-permute-start | bytes 6152 | tf_op jit(solution)/shard_map/ppermute | solution.py:33
  317.6 4.7 collective-permute-start.7
  319.5 2.7 copy-start.6
  461.6 55.2 %collective-permute-start = (bf16[512,1,128]{2,0,1:T(8,128)(2,1)}, bf16[512,1,128]{2,0,1:T(8,128)(2,1)S(1)}, u32[]{:S(2)}, u32[]{:S(2)}) collective-permute-start(bf16[512,1,128]{2,0,1:T(8,128)(2,1)} %get-tuple-element.6), channel_id=1, source_target_pairs={{0,8},{8,16},{16,24},{24,32},{32,40},{40,48},{48,56},{56,64},{64,7... | collective-permute-start | bytes 393224 | tf_op jit(solution)/shard_map/ppermute | solution.py:33
  467.3 49.4 %collective-permute-start.1 = (bf16[512,1,128]{2,0,1:T(8,128)(2,1)}, bf16[512,1,128]{2,0,1:T(8,128)(2,1)S(1)}, u32[]{:S(2)}, u32[]{:S(2)}) collective-permute-start(bf16[512,1,128]{2,0,1:T(8,128)(2,1)} %get-tuple-element.6), channel_id=1, source_target_pairs={{0,16},{8,24},{16,32},{24,40},{32,48},{40,56},{48,64},{56,72},{64,... | collective-permute-start | bytes 393224 | tf_op jit(solution)/shard_map/ppermute | solution.py:33
  470.4 46.3 %collective-permute-start.2 = (bf16[512,1,128]{2,0,1:T(8,128)(2,1)}, bf16[512,1,128]{2,0,1:T(8,128)(2,1)S(1)}, u32[]{:S(2)}, u32[]{:S(2)}) collective-permute-start(bf16[512,1,128]{2,0,1:T(8,128)(2,1)} %get-tuple-element.6), channel_id=1, source_target_pairs={{0,24},{8,32},{16,40},{24,48},{32,56},{40,64},{48,72},{56,80},{64,... | collective-permute-start | bytes 393224 | tf_op jit(solution)/shard_map/ppermute | solution.py:33
  475.0 14.3 %collective-permute-start.8 = (bf16[512,1,128]{2,0,1:T(8,128)(2,1)}, bf16[512,1,128]{2,0,1:T(8,128)(2,1)}, u32[]{:S(2)}, u32[]{:S(2)}) collective-permute-start(bf16[512,1,128]{2,0,1:T(8,128)(2,1)} %get-tuple-element.10), channel_id=1, source_target_pairs={{0,8},{8,16},{16,24},{24,32},{32,40},{40,48},{48,56},{56,64},{64,7... | collective-permute-start | bytes 393224 | tf_op jit(solution)/shard_map/ppermute | solution.py:33
  477.5 16.7 %collective-permute-start.9 = (bf16[512,1,128]{2,0,1:T(8,128)(2,1)}, bf16[512,1,128]{2,0,1:T(8,128)(2,1)}, u32[]{:S(2)}, u32[]{:S(2)}) collective-permute-start(bf16[512,1,128]{2,0,1:T(8,128)(2,1)} %get-tuple-element.10), channel_id=1, source_target_pairs={{0,16},{8,24},{16,32},{24,40},{32,48},{40,56},{48,64},{56,72},{64,... | collective-permute-start | bytes 393224 | tf_op jit(solution)/shard_map/ppermute | solution.py:33
  483.5 4.3 copy-start
  489.2 14.9 %copy-start.2 = (pred[512,2560]{0,1:T(8,128)(4,1)S(1)}, pred[512,2560]{0,1:T(8,128)(4,1)}, u32[]{:S(2)}) copy-start(pred[512,2560]{0,1:T(8,128)(4,1)} %and_and_fusion) | copy-start | bytes 3932164
  489.4 8.8 %collective-permute-start.10 = (bf16[512,1,128]{2,0,1:T(8,128)(2,1)}, bf16[512,1,128]{2,0,1:T(8,128)(2,1)S(1)}, u32[]{:S(2)}, u32[]{:S(2)}) collective-permute-start(bf16[512,1,128]{2,0,1:T(8,128)(2,1)} %get-tuple-element.10), channel_id=1, source_target_pairs={{0,24},{8,32},{16,40},{24,48},{32,56},{40,64},{48,72},{56,80},{64,... | collective-permute-start | bytes 393224 | tf_op jit(solution)/shard_map/ppermute | solution.py:33
  494.3 9.1 %collective-permute-start.11 = (bf16[512,1,128]{2,0,1:T(8,128)(2,1)}, bf16[512,1,128]{2,0,1:T(8,128)(2,1)S(1)}, u32[]{:S(2)}, u32[]{:S(2)}) collective-permute-start(bf16[512,1,128]{2,0,1:T(8,128)(2,1)} %get-tuple-element.10), channel_id=1, source_target_pairs={{0,32},{8,40},{16,48},{24,56},{32,64},{40,72},{48,80},{56,88},{64,... | collective-permute-start | bytes 393224 | tf_op jit(solution)/shard_map/ppermute | solution.py:33
  498.2 18.6 %collective-permute-start.3 = (bf16[512,1,128]{2,0,1:T(8,128)(2,1)}, bf16[512,1,128]{2,0,1:T(8,128)(2,1)S(1)}, u32[]{:S(2)}, u32[]{:S(2)}) collective-permute-start(bf16[512,1,128]{2,0,1:T(8,128)(2,1)} %get-tuple-element.6), channel_id=1, source_target_pairs={{0,32},{8,40},{16,48},{24,56},{32,64},{40,72},{48,80},{56,88},{64,... | collective-permute-start | bytes 393224 | tf_op jit(solution)/shard_map/ppermute | solution.py:33
  504.1 12.6 %copy-start.3 = (bf16[2560,1,128]{2,0,1:T(8,128)(2,1)S(1)}, bf16[2560,1,128]{2,0,1:T(8,128)(2,1)}, u32[]{:S(2)}) copy-start(bf16[2560,1,128]{2,0,1:T(8,128)(2,1)} %get-tuple-element.5) | copy-start | bytes 1966084
Sparse Core Ops, SparseCore 0:
  9.1 100.2 all-gather.2
  111.2 134.8 all-gather.4
  309.6 148.6 reduce-scatter.1
where the time goes:
time: 534 us; the launch traced here: 533 us
  waiting for transfers between devices  262 us (49%)
  blocking collectives  123 us (23%)
  starting transfers between devices  54.4 us (10%)
  matrix products  40.8 us (8%)
  other arithmetic  21.9 us (4%)
  local copies, waits for them, and re-layouts  16.3 us (3%)
  between operations  14.4 us (3%)
    reduce_scatter x1, waiting for transfers between devices, on_device(): lax.psum_scatter(partial_value.astype(jnp.bfloat16), 'wt', scatter_dimens...  132 us
    all_to_all x1, waiting for transfers between devices, summed_on_arrival(): lax.all_to_all(parts, axis, split_axis=0, concat_axis=0, tiled=True)  74.6 us
    all_gather x1, blocking collectives, on_device(): lax.all_gather(llm_scales, 'ctx', axis=2, tiled=True)  54.9 us
    all_gather x1, waiting for transfers between devices, merge_project(): codes_piece = lax.all_gather(merger_codes, 'ctx', axis=2, tiled=True)  47.2 us
    all_gather x1, blocking collectives, merge_project(): scale_piece = lax.all_gather(merger_scales, 'ctx', axis=2, tiled=True)  45.9 us
    ppermute x12, starting transfers between devices, passed_along(): lax.ppermute(value, axis, [(source, source + steps) for source in range(l...  37.9 us
    psum x1, blocking collectives, on_device(): squares = lax.psum(jnp.sum(values * values, axis=1), 'wt')  22.5 us
    sub x2, matrix products, softmax_rows(): raised = jnp.exp(masked - highest)  13.6 us
  transfers between devices with their start and end apart: 18, of which 4 were waited for; matrix products, arithmetic and copies ran while one was open for 10% of the time, Pallas kernels for 0%

commit v1 on v0

--- a/solution.py
+++ b/solution.py
@@ -14,6 +14,12 @@
 RMS_EPS = 1e-06
 ROPE_BASE = 1000000.0
 FILL_LOW = -1e30
+
+
+def cycles_draw(shard_axis, own_rows):
+    return jnp.concatenate(
+        lax.all_to_all(jnp.stack(lax.axis_size(shard_axis) * [own_rows], 0), shard_axis, 0, 0), 2
+    )
 
 
 def in_blocks(x, dim, peers):
@@ -154,7 +160,7 @@
 ):
     early_codes, early_scales = (
         lax.all_gather(llm_codes, "ctx", axis=2, tiled=True),
-        lax.all_gather(llm_scales, "ctx", axis=2, tiled=True),
+        cycles_draw("ctx", llm_scales),
     )
     row_count = text_embed.shape[0]
     first = lax.axis_index("ctx") * row_count

time: 534 us -> 509 us (0.953)
  blocking collectives: 123 us -> 70.1 us
  waiting for transfers between devices: 262 us -> 280 us
  starting transfers between devices: 54.4 us -> 64.5 us
    all_gather x1 -> x0, blocking collectives: 54.9 us -> none  [on_device(): lax.all_gather(llm_scales, 'ctx', axis=2, tiled=True)]
    all_to_all x1, waiting for transfers between devices: 0.01 us -> 15.9 us  [route_tokens(): lax.all_to_all(packed, 'ctx', split_axis=0, concat_axis=0, tiled=True)]
    all_to_all x0 -> x1, waiting for transfers between devices: none -> 7.87 us  [cycles_draw(): lax.all_to_all(jnp.stack(lax.axis_size(shard_axis) * [own_rows], 0), shar...]
    reduce_scatter x1, waiting for transfers between devices: 132 us -> 126 us  [on_device(): lax.psum_scatter(partial_value.astype(jnp.bfloat16), 'wt', scatter_dimens...]
    ppermute x12, starting transfers between devices: 37.9 us -> 44.3 us  [passed_along(): lax.ppermute(value, axis, [(source, source + steps) for source in range(l...]
  transfers between devices with their start and end apart: 18 -> 19, of which waited for: 4 -> 6; matrix products, arithmetic and copies ran while one was open for 10% -> 11% of each run, Pallas kernels for 0% -> 0%
where the time goes in v1:
time: 509 us; the launch traced here: 508 us
  waiting for transfers between devices  280 us (55%)
  blocking collectives  70.1 us (14%)
  starting transfers between devices  64.5 us (13%)
  matrix products  40.8 us (8%)
  other arithmetic  21.5 us (4%)
  local copies, waits for them, and re-layouts  16.9 us (3%)
  between operations  14.4 us (3%)
    reduce_scatter x1, waiting for transfers between devices, on_device(): lax.psum_scatter(partial_value.astype(jnp.bfloat16), 'wt', scatter_dimens...  126 us
    all_to_all x1, waiting for transfers between devices, summed_on_arrival(): lax.all_to_all(parts, axis, split_axis=0, concat_axis=0, tiled=True)  74.6 us
    all_gather x1, waiting for transfers between devices, merge_project(): codes_piece = lax.all_gather(merger_codes, 'ctx', axis=2, tiled=True)  47.2 us
    all_gather x1, blocking collectives, merge_project(): scale_piece = lax.all_gather(merger_scales, 'ctx', axis=2, tiled=True)  45.9 us
    ppermute x12, starting transfers between devices, passed_along(): lax.ppermute(value, axis, [(source, source + steps) for source in range(l...  44.3 us
    psum x1, blocking collectives, on_device(): squares = lax.psum(jnp.sum(values * values, axis=1), 'wt')  24.2 us
    all_to_all x1, waiting for transfers between devices, route_tokens(): lax.all_to_all(packed, 'ctx', split_axis=0, concat_axis=0, tiled=True)  15.9 us
    sub x2, matrix products, softmax_rows(): raised = jnp.exp(masked - highest)  13.6 us
  transfers between devices with their start and end apart: 19, of which 6 were waited for; matrix products, arithmetic and copies ran while one was open for 11% of the time, Pallas kernels for 0%

profile of v1, /device:TPU:1, one launch (start us, length us, event | category | flops | bytes accessed | tf_op | source)
XLA Modules:
  0.0 508.3 jit_solution(10059325627666861314)
XLA Ops:
  11.3 2.2 fusion.29
  16.2 45.9 %all_gather.10 = bf16[1,1,8192]{2,1,0:T(2,128)(2,1)S(1)} all-gather(bf16[1,1,256]{2,1,0:T(2,128)(2,1)S(1)} %copy-done.8), channel_id=1, replica_groups=mesh['ctx'=32,'wt'=8] {'ctx'}, dimensions={2}, use_global_device_ids=true | all-gather | bytes 16896 | tf_op jit(solution)/shard_map/all_gather | solution.py:103
  62.2 47.2 %all-gather.3.cloned.1.call-done = bf16[4,160,8192]{2,1,0:T(8,128)(2,1)} async-done(((bf16[4,160,256]{2,1,0:T(8,128)(2,1)}), bf16[4,160,8192]{2,1,0:T(8,128)(2,1)}) %all-gather.3.cloned.1.call-update) | async-done | bytes 10485776 | tf_op jit(solution)/shard_map/all_gather | solution.py:102
  109.4 6.2 %multiply_convert_fusion.1 = bf16[4,160,8192]{2,1,0:T(8,128)(2,1)S(1)} fusion(bf16[4,160,8192]{2,1,0:T(8,128)(2,1)} %all-gather.3.cloned.1.call-done, f32[8192]{0:T(1024)S(1)} %bitcast.113), kind=kLoop, calls=%fused_computation.6 | loop fusion | flops 15728640 | bytes 21004288 | tf_op jit(solution)/shard_map/convert_element_type | solution.py:105
  115.6 2.0 convolution_convert_fusion
  119.1 7.4 %all-to-all-start.1 = ((bf16[8,128,1024]{2,1,0:T(8,128)(2,1)}), bf16[8,128,1024]{2,1,0:T(8,128)(2,1)S(1)}, u32[]{:S(2)}, u32[]{:S(2)}) async-start(bf16[8,128,1024]{2,1,0:T(8,128)(2,1)} %bitcast.106), calls=%async_computation.1 | async-start | bytes 4194304 | tf_op jit(solution)/shard_map/all_to_all | solution.py:32
  127.6 74.6 %all-to-all-done.1 = bf16[8,128,1024]{2,1,0:T(8,128)(2,1)S(1)} async-done(((bf16[8,128,1024]{2,1,0:T(8,128)(2,1)}), bf16[8,128,1024]{2,1,0:T(8,128)(2,1)S(1)}, u32[]{:S(2)}, u32[]{:S(2)}) %all-to-all-start.1) | async-done | bytes 2097184 | tf_op jit(solution)/shard_map/all_to_all | solution.py:32
  202.2 4.9 all-to-all-start
  207.5 7.1 %all-to-all-done = s32[32,8,1]{1,2,0:T(1,128)S(1)} async-done(((s32[32,8,1]{1,2,0:T(1,128)}), s32[32,8,1]{1,2,0:T(1,128)S(1)}, u32[]{:S(2)}, u32[]{:S(2)}) %all-to-all-start) | async-done | bytes 1056 | tf_op jit(solution)/shard_map/all_to_all | solution.py:129
  215.2 4.0 all-to-all-start.3
  220.3 7.9 %all-to-all-done.3 = bf16[32,1,8,24]{3,2,1,0:T(8,128)(2,1)S(1)} async-done(((bf16[32,1,8,24]{3,2,1,0:T(8,128)(2,1)}), bf16[32,1,8,24]{3,2,1,0:T(8,128)(2,1)S(1)}, u32[]{:S(2)}, u32[]{:S(2)}) %all-to-all-start.3) | async-done | bytes 12320 | tf_op jit(solution)/shard_map/all_to_all | solution.py:21
  228.2 3.7 all-to-all-start.2
  232.4 15.9 %all-to-all-done.2 = bf16[32,8,1024]{2,1,0:T(8,128)(2,1)S(1)} async-done(((bf16[32,8,1024]{2,1,0:T(8,128)(2,1)}), bf16[32,8,1024]{2,1,0:T(8,128)(2,1)S(1)}, u32[]{:S(2)}, u32[]{:S(2)}) %all-to-all-start.2) | async-done | bytes 524320 | tf_op jit(solution)/shard_map/all_to_all | solution.py:128
  248.9 24.2 %psum.7 = f32[512]{0:T(512)S(1)} all-reduce(f32[512]{0:T(512)S(1)} %get-tuple-element.24), channel_id=1, replica_groups=mesh['ctx'=32,'wt'=8] {'wt'}, use_global_device_ids=true, to_apply=%region_8.9 | all-reduce | flops 512 | bytes 4096 | tf_op jit(solution)/shard_map/psum | solution.py:178
  273.1 11.6 %fusion.11 = bf16[512,8,768]{2,0,1:T(8,128)(2,1)} fusion(bf16[1024,8,768]{0,2,1:T(8,128)(2,1)} %all-gather.5.cloned.1.call-done, f32[8,768]{1,0:T(8,128)S(1)} %reshape.482, bf16[512,1024]{1,0:T(8,128)(2,1)S(1)} %get-tuple-element.25, f32[1024]{0:T(1024)S(1)} %copy-done.12, f32[512]{0:T(512)S(1)} %add_rsqrt_fusion), kind=kOutput, calls=%fused_computation.18 | convolution fusion | flops 6466568192 | bytes 19953664 | tf_op jit(solution)/shard_map/dot_general | solution.py:184
  285.4 7.1 %collective-permute-start.4 = (s32[512]{0:T(512)S(1)}, s32[512]{0:T(512)S(1)}, u32[]{:S(2)}, u32[]{:S(2)}) collective-permute-start(s32[512]{0:T(512)S(1)} %copy-done.4), channel_id=1, source_target_pairs={{0,8},{8,16},{16,24},{24,32},{32,40},{40,48},{48,56},{56,64},{64,7... | collective-permute-start | bytes 6152 | tf_op jit(solution)/shard_map/ppermute | solution.py:39
  294.2 3.4 collective-permute-start.6
  297.7 3.4 collective-permute-start.7
  304.2 3.5 and_and_fusion
  307.6 126.0 %reduce-scatter.2.cloned.1.call-done = bf16[512,1,768]{2,0,1:T(8,128)(2,1)} async-done(((bf16[512,8,768]{2,0,1:T(8,128)(2,1)}), bf16[512,1,768]{2,0,1:T(8,128)(2,1)}) %reduce-scatter.2.cloned.1.call-update) | async-done | bytes 786448 | tf_op jit(solution)/shard_map/reduce_scatter | solution.py:188
  435.0 1.9 constant_dynamic-update-slice_fusion.4
  436.9 5.7 %collective-permute-start = (bf16[512,1,128]{2,0,1:T(8,128)(2,1)}, bf16[512,1,128]{2,0,1:T(8,128)(2,1)S(1)}, u32[]{:S(2)}, u32[]{:S(2)}) collective-permute-start(bf16[512,1,128]{2,0,1:T(8,128)(2,1)} %get-tuple-element.6), channel_id=1, source_target_pairs={{0,8},{8,16},{16,24},{24,32},{32,40},{40,48},{48,56},{56,64},{64,7... | collective-permute-start | bytes 393224 | tf_op jit(solution)/shard_map/ppermute | solution.py:39
  442.6 3.1 collective-permute-start.1
  445.8 3.4 collective-permute-start.2
  450.3 2.5 collective-permute-start.8
  452.9 3.8 collective-permute-start.9
  460.5 2.6 mul.216
  464.7 3.3 collective-permute-start.10
  469.6 2.4 collective-permute-start.11
  473.6 4.5 collective-permute-start.3
  479.4 12.6 %fusion.83 = (f32[4,512]{1,0:T(4,128)S(1)}, f32[4,512,2560]{1,2,0:T(8,128)}) fusion(pred[512,2560]{0,1:T(8,128)(4,1)S(1)} %copy-done.2, bf16[2560,1,128]{2,0,1:T(8,128)(2,1)} %constant_dynamic-update-slice_fusion.7, bf16[512,4,128]{2,1,0:T(4,128)(2,1)S(1)} %convert_element_type.149), kind=kOutput, calls=%fused_computation.138 | convolution fusion | flops 1363151360 | bytes 23470080 | tf_op jit(solution)/shard_map/sub | solution.py:45
  492.2 8.5 %fusion.28 = bf16[128,4,512]{2,0,1:T(8,128)(2,1)S(1)} fusion(f32[4,512,2560]{1,2,0:T(8,128)} %get-tuple-element.27, f32[4,512]{1,0:T(4,128)S(1)} %get-tuple-element.26, bf16[2560,1,128]{2,0,1:T(8,128)(2,1)S(1)} %constant_dynamic-update-slice_fusion), kind=kOutput, calls=%fused_computation.44 | convolution fusion | flops 1352925184 | bytes 22159360 | tf_op jit(solution)/shard_map/jqk,kd->qjd/dot_general | solution.py:219
  (112 shorter events, 31.3 us)
Async XLA Ops:
  6.5 4.8 copy-start.1
  6.5 4.8 copy-start.10
  6.5 4.8 copy-start.11
  6.5 102.9 %all-gather.3.cloned.1.call-start = ((), (), s32[]{:S(2)}) async-start(), calls=%async_computation.5 | async-start | bytes 10813440 | tf_op jit(solution)/shard_map/all_gather | solution.py:102
  7.3 265.8 %all-gather.5.cloned.1.call-start = ((), (), s32[]{:S(2)}) async-start(), calls=%async_computation.6 | async-start | bytes 12976128 | tf_op jit(solution)/shard_map/all_gather | solution.py:162
  14.6 1.6 copy-start.8
  119.1 7.4 %copy-start.13 = (s32[128]{0:T(128)S(1)}, s32[128]{0:T(128)}, u32[]{:S(2)}) copy-start(s32[128]{0:T(128)} %param.25) | copy-start | bytes 1540
  119.1 83.1 %all-to-all-start.1 = ((bf16[8,128,1024]{2,1,0:T(8,128)(2,1)}), bf16[8,128,1024]{2,1,0:T(8,128)(2,1)S(1)}, u32[]{:S(2)}, u32[]{:S(2)}) async-start(bf16[8,128,1024]{2,1,0:T(8,128)(2,1)} %bitcast.106), calls=%async_computation.1 | async-start | bytes 4194304 | tf_op jit(solution)/shard_map/all_to_all | solution.py:32
  126.5 88.0 %copy-start.7 = (bf16[1,8,24]{2,1,0:T(8,128)(2,1)S(1)}, bf16[1,8,24]{2,1,0:T(8,128)(2,1)}, u32[]{:S(2)}) copy-start(bf16[1,8,24]{2,1,0:T(8,128)(2,1)} %param.29) | copy-start | bytes 1156
  126.5 92.7 %copy-start.5 = (f32[1024]{0:T(1024)S(1)}, f32[1024]{0:T(1024)}, u32[]{:S(2)}) copy-start(f32[1024]{0:T(1024)} %param.24) | copy-start | bytes 12292
  202.2 12.4 %all-to-all-start = ((s32[32,8,1]{1,2,0:T(1,128)}), s32[32,8,1]{1,2,0:T(1,128)S(1)}, u32[]{:S(2)}, u32[]{:S(2)}) async-start(s32[32,8,1]{1,2,0:T(1,128)} %bitcast), calls=%async_computation | async-start | bytes 32768 | tf_op jit(solution)/shard_map/all_to_all | solution.py:129
  207.5 40.8 %copy-start.9 = (bf16[512,1024]{1,0:T(8,128)(2,1)S(1)}, bf16[512,1024]{1,0:T(8,128)(2,1)}, u32[]{:S(2)}) copy-start(bf16[512,1024]{1,0:T(8,128)(2,1)} %param.26) | copy-start | bytes 3145732
  215.2 13.0 %all-to-all-start.3 = ((bf16[32,1,8,24]{3,2,1,0:T(8,128)(2,1)}), bf16[32,1,8,24]{3,2,1,0:T(8,128)(2,1)S(1)}, u32[]{:S(2)}, u32[]{:S(2)}) async-start(bf16[32,1,8,24]{3,2,1,0:T(8,128)(2,1)} %stack.2), calls=%async_computation.3 | async-start | bytes 131072 | tf_op jit(solution)/shard_map/all_to_all | solution.py:21
  228.2 20.1 %all-to-all-start.2 = ((bf16[32,8,1024]{2,1,0:T(8,128)(2,1)}), bf16[32,8,1024]{2,1,0:T(8,128)(2,1)S(1)}, u32[]{:S(2)}, u32[]{:S(2)}) async-start(bf16[32,8,1024]{2,1,0:T(8,128)(2,1)} %fusion.32), calls=%async_computation.2 | async-start | bytes 1048576 | tf_op jit(solution)/shard_map/all_to_all | solution.py:128
  231.9 201.7 %reduce-scatter.2.cloned.1.call-start = ((), (), s32[]{:S(2)}) async-start(), calls=%async_computation.7 | async-start | bytes 7077888 | tf_op jit(solution)/shard_map/reduce_scatter | solution.py:188
  232.2 40.9 %copy-start.12 = (f32[1024]{0:T(1024)S(1)}, f32[1024]{0:T(1024)}, u32[]{:S(2)}) copy-start(f32[1024]{0:T(1024)} %param.27) | copy-start | bytes 12292
  285.4 18.7 %collective-permute-start.4 = (s32[512]{0:T(512)S(1)}, s32[512]{0:T(512)S(1)}, u32[]{:S(2)}, u32[]{:S(2)}) collective-permute-start(s32[512]{0:T(512)S(1)} %copy-done.4), channel_id=1, source_target_pairs={{0,8},{8,16},{16,24},{24,32},{32,40},{40,48},{48,56},{56,64},{64,7... | collective-permute-start | bytes 6152 | tf_op jit(solution)/shard_map/ppermute | solution.py:39
  292.6 11.6 %collective-permute-start.5 = (s32[512]{0:T(512)S(1)}, s32[512]{0:T(512)S(1)}, u32[]{:S(2)}, u32[]{:S(2)}) collective-permute-start(s32[512]{0:T(512)S(1)} %copy-done.4), channel_id=1, source_target_pairs={{0,16},{8,24},{16,32},{24,40},{32,48},{40,56},{48,64},{56,72},{64,... | collective-permute-start | bytes 6152 | tf_op jit(solution)/shard_map/ppermute | solution.py:39
  294.2 9.9 %collective-permute-start.6 = (s32[512]{0:T(512)S(1)}, s32[512]{0:T(512)S(1)}, u32[]{:S(2)}, u32[]{:S(2)}) collective-permute-start(s32[512]{0:T(512)S(1)} %copy-done.4), channel_id=1, source_target_pairs={{0,24},{8,32},{16,40},{24,48},{32,56},{40,64},{48,72},{56,80},{64,... | collective-permute-start | bytes 6152 | tf_op jit(solution)/shard_map/ppermute | solution.py:39
  297.7 6.5 %collective-permute-start.7 = (s32[512]{0:T(512)S(1)}, s32[512]{0:T(512)S(1)}, u32[]{:S(2)}, u32[]{:S(2)}) collective-permute-start(s32[512]{0:T(512)S(1)} %copy-done.4), channel_id=1, source_target_pairs={{0,32},{8,40},{16,48},{24,56},{32,64},{40,72},{48,80},{56,88},{64,... | collective-permute-start | bytes 6152 | tf_op jit(solution)/shard_map/ppermute | solution.py:39
  301.3 2.7 copy-start.6
  436.9 55.1 %collective-permute-start = (bf16[512,1,128]{2,0,1:T(8,128)(2,1)}, bf16[512,1,128]{2,0,1:T(8,128)(2,1)S(1)}, u32[]{:S(2)}, u32[]{:S(2)}) collective-permute-start(bf16[512,1,128]{2,0,1:T(8,128)(2,1)} %get-tuple-element.6), channel_id=1, source_target_pairs={{0,8},{8,16},{16,24},{24,32},{32,40},{40,48},{48,56},{56,64},{64,7... | collective-permute-start | bytes 393224 | tf_op jit(solution)/shard_map/ppermute | solution.py:39
  442.6 49.4 %collective-permute-start.1 = (bf16[512,1,128]{2,0,1:T(8,128)(2,1)}, bf16[512,1,128]{2,0,1:T(8,128)(2,1)S(1)}, u32[]{:S(2)}, u32[]{:S(2)}) collective-permute-start(bf16[512,1,128]{2,0,1:T(8,128)(2,1)} %get-tuple-element.6), channel_id=1, source_target_pairs={{0,16},{8,24},{16,32},{24,40},{32,48},{40,56},{48,64},{56,72},{64,... | collective-permute-start | bytes 393224 | tf_op jit(solution)/shard_map/ppermute | solution.py:39
  445.8 46.4 %collective-permute-start.2 = (bf16[512,1,128]{2,0,1:T(8,128)(2,1)}, bf16[512,1,128]{2,0,1:T(8,128)(2,1)S(1)}, u32[]{:S(2)}, u32[]{:S(2)}) collective-permute-start(bf16[512,1,128]{2,0,1:T(8,128)(2,1)} %get-tuple-element.6), channel_id=1, source_target_pairs={{0,24},{8,32},{16,40},{24,48},{32,56},{40,64},{48,72},{56,80},{64,... | collective-permute-start | bytes 393224 | tf_op jit(solution)/shard_map/ppermute | solution.py:39
  450.3 14.4 %collective-permute-start.8 = (bf16[512,1,128]{2,0,1:T(8,128)(2,1)}, bf16[512,1,128]{2,0,1:T(8,128)(2,1)}, u32[]{:S(2)}, u32[]{:S(2)}) collective-permute-start(bf16[512,1,128]{2,0,1:T(8,128)(2,1)} %get-tuple-element.10), channel_id=1, source_target_pairs={{0,8},{8,16},{16,24},{24,32},{32,40},{40,48},{48,56},{56,64},{64,7... | collective-permute-start | bytes 393224 | tf_op jit(solution)/shard_map/ppermute | solution.py:39
  452.9 16.7 %collective-permute-start.9 = (bf16[512,1,128]{2,0,1:T(8,128)(2,1)}, bf16[512,1,128]{2,0,1:T(8,128)(2,1)}, u32[]{:S(2)}, u32[]{:S(2)}) collective-permute-start(bf16[512,1,128]{2,0,1:T(8,128)(2,1)} %get-tuple-element.10), channel_id=1, source_target_pairs={{0,16},{8,24},{16,32},{24,40},{32,48},{40,56},{48,64},{56,72},{64,... | collective-permute-start | bytes 393224 | tf_op jit(solution)/shard_map/ppermute | solution.py:39
  458.8 4.3 copy-start
  464.6 14.8 %copy-start.2 = (pred[512,2560]{0,1:T(8,128)(4,1)S(1)}, pred[512,2560]{0,1:T(8,128)(4,1)}, u32[]{:S(2)}) copy-start(pred[512,2560]{0,1:T(8,128)(4,1)} %and_and_fusion) | copy-start | bytes 3932164
  464.7 8.8 %collective-permute-start.10 = (bf16[512,1,128]{2,0,1:T(8,128)(2,1)}, bf16[512,1,128]{2,0,1:T(8,128)(2,1)S(1)}, u32[]{:S(2)}, u32[]{:S(2)}) collective-permute-start(bf16[512,1,128]{2,0,1:T(8,128)(2,1)} %get-tuple-element.10), channel_id=1, source_target_pairs={{0,24},{8,32},{16,40},{24,48},{32,56},{40,64},{48,72},{56,80},{64,... | collective-permute-start | bytes 393224 | tf_op jit(solution)/shard_map/ppermute | solution.py:39
  469.6 9.2 %collective-permute-start.11 = (bf16[512,1,128]{2,0,1:T(8,128)(2,1)}, bf16[512,1,128]{2,0,1:T(8,128)(2,1)S(1)}, u32[]{:S(2)}, u32[]{:S(2)}) collective-permute-start(bf16[512,1,128]{2,0,1:T(8,128)(2,1)} %get-tuple-element.10), channel_id=1, source_target_pairs={{0,32},{8,40},{16,48},{24,56},{32,64},{40,72},{48,80},{56,88},{64,... | collective-permute-start | bytes 393224 | tf_op jit(solution)/shard_map/ppermute | solution.py:39
  473.6 18.6 %collective-permute-start.3 = (bf16[512,1,128]{2,0,1:T(8,128)(2,1)}, bf16[512,1,128]{2,0,1:T(8,128)(2,1)S(1)}, u32[]{:S(2)}, u32[]{:S(2)}) collective-permute-start(bf16[512,1,128]{2,0,1:T(8,128)(2,1)} %get-tuple-element.6), channel_id=1, source_target_pairs={{0,32},{8,40},{16,48},{24,56},{32,64},{40,72},{48,80},{56,88},{64,... | collective-permute-start | bytes 393224 | tf_op jit(solution)/shard_map/ppermute | solution.py:39
  479.4 12.6 %copy-start.3 = (bf16[2560,1,128]{2,0,1:T(8,128)(2,1)S(1)}, bf16[2560,1,128]{2,0,1:T(8,128)(2,1)}, u32[]{:S(2)}) copy-start(bf16[2560,1,128]{2,0,1:T(8,128)(2,1)} %get-tuple-element.5) | copy-start | bytes 1966084
  (1 other events, 0.7 us)
Sparse Core Ops, SparseCore 0:
  9.1 100.2 all-gather.2
  111.2 124.3 all-gather.4
  284.9 148.6 reduce-scatter.1
